TPU v7x, 32 devices: a whole 2x2x4 slice. The times are simulated.
32 devices in a mesh: batch: 4 (over x, core), centers: 8 (over z, y).
Axes of the slice: x: 2, y: 2, z: 4, core: 2. Of those that a mesh axis runs over, the one named last changes fastest.
Arguments:
- pool_features: float32 [32768, 128], P(('batch', 'centers')), may hold values from -14 to 14
- pool_targets: float32 [32768, 64], P(('batch', 'centers')), may hold values from -6 to 6
- batch_index: int32 [2048], P(('batch', 'centers')), may hold values from 0 to 1023
- centers: float32 [4096, 128], P('centers'), may hold values from -14 to 14
- weights: float32 [4096, 64], P('centers'), as said below
- eig_vectors: float32 [4096, 1024], P(('batch', 'centers')), may hold values from -0.09375 to 0.09375
- eig_scale: float32 [1024], replicated, may hold values from 0.5 to 4
- nys_owner: int32 [4096, 1], P(('batch', 'centers')), may hold values from 0 to 7; in each aligned block of 128 rows (0 to 127, 128 to 255, ...) at most 32 rows name the same one
- nys_offset: int32 [4096], P(('batch', 'centers')), may hold values from 0 to 511
Outputs:
- residual_out: float32 [2048, 64], P(('batch', 'centers'))
- update: float32 [4096, 64], P('centers')
Inputs may be any that keep to these rules, and one draw needn't show every extreme that they name: `nys_owner`: among the 128 rows of one device no owner is named more than 32 times; on some devices one owner is named exactly 32 times. `weights`: every column sums to zero.
All inputs are finite; a program needn't handle non-finite values.
Results may differ from a plain program's by a relative error of at most 0.0003.
Values sent between devices are 32-bit elements; how exact they have to be, the bound alone decides.
A program may use at most 64 MiB of HBM per device.

v0:
```python
import functools
import math

import jax
import jax.numpy as jnp
from jax import lax
from jax.experimental import pallas as pl
from jax.experimental.pallas import tpu as pltpu
from jax.sharding import PartitionSpec as P

DEPTH = 3
EPS = 1e-06
HIGH = lax.Precision.HIGHEST
MESH = pl.DeviceIdType.MESH
FIRST, EACH, EARLY = 16, 0, 1
ACOS = (
    1.5707963050,
    -0.2145988016,
    0.0889789874,
    -0.0501743046,
    0.0308918810,
    -0.0170881256,
    0.0066700901,
    -0.0012624911,
)


def dot(a, b, ca, cb):
    return lax.dot_general(
        a,
        b,
        (((ca,), (cb,)), ((), ())),
        precision=HIGH,
        preferred_element_type=jnp.float32,
    )


def pick(onehot, x):
    low = jnp.bfloat16
    hi = x.astype(low)
    rest = x - hi.astype(jnp.float32)
    mid = rest.astype(low)
    parts = (rest - mid.astype(jnp.float32)).astype(low), mid, hi
    total = None
    for p in parts:
        part = jnp.dot(onehot, p, preferred_element_type=jnp.float32)
        total = part if total is None else total + part
    return total


def fold(x):
    h = x.shape[0] // 2
    return jnp.concatenate([x[:h], x[h:]], axis=1)


def unfold(x):
    h = x.shape[1] // 2
    return jnp.concatenate([x[:, :h], x[:, h:]], axis=0)


def arc_parts(x):
    u = jnp.maximum(1.0 - x, 1e-30)
    poly = jnp.full_like(x, ACOS[-1] / math.pi)
    for a in ACOS[-2::-1]:
        poly = poly * x + a / math.pi
    v = u * (1.0 + x)
    return u * lax.rsqrt(u) * poly, v * lax.rsqrt(v) * (1.0 / math.pi)


def tangent_kernel(cosine):
    arc, sine = arc_parts(jnp.abs(cosine))
    remain = jnp.where(cosine < 0.0, arc, 1.0 - arc)
    prod = remain * cosine
    sigma = sine + prod
    tangent = sigma + prod
    for _ in range(DEPTH - 1):
        arc, sine = arc_parts(sigma)
        remain = 1.0 - arc
        sigma = sine + remain * sigma
        tangent = sigma + tangent * remain
    return tangent


def body(
    nb,
    nc,
    pool_f,
    pool_t,
    index,
    cen,
    wts,
    eig,
    scale,
    owner,
    offset,
    res_out,
    upd_out,
    feat,
    feat_all,
    kbuf,
    ppart,
    prx,
    rsend,
    rrx,
    packed,
    eigrx,
    offsend,
    offrx,
    ebar,
    gsend,
    grx,
    gown,
    gall,
    csend,
    crx,
    cown,
    call,
    usend,
    urx,
    uown,
    uall,
    f_s,
    f_r,
    p_s,
    p_r,
    r_s,
    r_r,
    e_s,
    e_r,
    o_s,
    o_r,
    g_s,
    g_r,
    ga_s,
    ga_r,
    c_s,
    c_r,
    ca_s,
    ca_r,
    u_s,
    u_r,
    ua_s,
    ua_r,
):
    b = lax.axis_index("batch")
    c = lax.axis_index("centers")
    n = nb * nc
    me = b * nc + c
    rows, dim = feat.shape
    cdev = cen.shape[0]
    pts = owner.shape[1]
    slots = packed.shape[1] // nc
    qb = packed.shape[2]
    piece = cdev // nb
    rows_total = rows * n

    def copy(src, dst, ssem, rsem, db, dc):
        return pltpu.make_async_remote_copy(
            src_ref=src,
            dst_ref=dst,
            send_sem=ssem,
            recv_sem=rsem,
            device_id=(db, dc),
            device_id_type=MESH,
        )

    barrier = pltpu.get_barrier_semaphore()

    @pl.loop(1, n)
    def _(k):
        d = lax.rem(me + k, n)
        pl.semaphore_signal(
            barrier, inc=1, device_id=(lax.div(d, nc), lax.rem(d, nc)), device_id_type=MESH
        )

    drawn = (
        lax.broadcasted_iota(jnp.int32, (pool_f.shape[0], rows), 0) == index[...]
    ).astype(jnp.float32)
    feat[...] = dot(drawn, pool_f[...], 0, 0)
    cval = cen[...]
    csq = cval * cval
    ncol = jnp.mean(csq, axis=1, keepdims=True) + EPS
    sb_col = jnp.sqrt(ncol)
    chat = cval / (sb_col * dim)
    sb_row = jnp.sqrt(dot(jnp.full((8, dim), 1.0 / dim, jnp.float32), csq, 1, 1)[0:1] + EPS)
    wb = wts[...] * sb_row
    a = feat[...]
    sa = jnp.sqrt(jnp.mean(a * a, axis=1, keepdims=True) + EPS)

    own = owner[...]
    hot = (own == lax.broadcasted_iota(jnp.int32, (nc, pts), 0)).astype(jnp.float32)
    upper = (
        lax.broadcasted_iota(jnp.int32, (pts, pts), 0)
        < lax.broadcasted_iota(jnp.int32, (pts, pts), 1)
    ).astype(jnp.float32)
    rank = jnp.sum(dot(hot, upper, 1, 0) * hot, axis=0, keepdims=True).astype(jnp.int32)
    spots = lax.broadcasted_iota(jnp.int32, (nc * slots, pts), 0)
    place = (spots == own * slots + rank).astype(jnp.float32)
    rowsp = dot(place, eig[...], 1, 0)
    for j in range(nb):
        packed[j] = rowsp[:, j * qb : (j + 1) * qb]
    here = (spots == c * slots + rank).astype(jnp.float32)
    marks = dot(hot * (offset[...].astype(jnp.float32) + 1.0), here, 1, 1)
    for j in range(nc):
        offsend[j] = marks[j : j + 1]

    eigrx[me] = packed[b, pl.ds(pl.multiple_of(c * slots, slots), slots)]
    offrx[me] = offsend[c]

    targ = dot(pool_t[...], drawn, 1, 0).T

    def block(av):
        na = jnp.mean(av * av, axis=1, keepdims=True) + EPS
        k = tangent_kernel(dot(av * lax.rsqrt(na), chat, 1, 1))
        return k, fold(dot(k, wb, 1, 1))

    kown, pown = block(a)
    kbuf[c] = kown
    prx[c] = pown

    pl.semaphore_wait(barrier, n - 1)

    def f_copy(k):
        return copy(feat, feat_all.at[c], f_s.at[k], f_r.at[c], b, lax.rem(c + k, nc))

    @pl.loop(1, nc)
    def _(k):
        f_copy(k).start()

    def e_copy(t):
        db, dc = lax.rem(b + lax.div(t, nc), nb), lax.rem(c + lax.rem(t, nc), nc)
        return copy(
            packed.at[db, pl.ds(pl.multiple_of(dc * slots, slots), slots)],
            eigrx.at[me],
            e_s.at[t],
            e_r.at[me],
            db,
            dc,
        )

    def o_copy(t):
        db, dc = lax.rem(b + lax.div(t, nc), nb), lax.rem(c + lax.rem(t, nc), nc)
        return copy(offsend.at[dc], offrx.at[me], o_s.at[t], o_r.at[me], db, dc)

    first = (n - 1) * FIRST // 32
    each = (n - 1) * EACH // (32 * (nc - 1))
    last = first + each * (nc - 1)

    @pl.loop(1, 1 + first)
    def _(t):
        e_copy(t).start()

    def p_copy(k):
        s = lax.rem(c - k + nc, nc)
        return copy(ppart.at[s], prx.at[c], p_s.at[k], p_r.at[c], b, s)

    @pl.loop(1, nc)
    def _(k):
        s = lax.rem(c - k + nc, nc)
        copy(feat, feat_all.at[s], f_s.at[k], f_r.at[s], b, s).wait_recv()
        kv, pv = block(feat_all[s])
        kbuf[s] = kv
        ppart[s] = pv
        p_copy(k).start()

        @pl.loop(0, each)
        def _(t):
            e_copy(1 + first + (k - 1) * each + t).start()

    @pl.loop(1, nc)
    def _(k):
        s = lax.rem(c + k, nc)
        copy(ppart.at[s], prx.at[s], p_s.at[k], p_r.at[s], b, s).wait_recv()

    pred = prx[0]
    for j in range(1, nc):
        pred = pred + prx[j]
    resid = unfold(pred) * sa - targ
    rs = resid * (sa / math.sqrt(rows_total))
    folded = fold(rs)
    rsend[...] = folded
    rrx[c] = folded

    def r_copy(k):
        return copy(rsend, rrx.at[c], r_s.at[k], r_r.at[c], b, lax.rem(c + k, nc))

    @pl.loop(1, nc)
    def _(k):
        r_copy(k).start()

    @pl.loop(1, n)
    def _(t):
        o_copy(t).start()

    @pl.loop(1 + last, n)
    def _(t):
        e_copy(t).start()

    res_out[...] = resid

    @pl.loop(1, nc)
    def _(k):
        s = lax.rem(c - k + nc, nc)
        copy(rsend, rrx.at[s], r_s.at[k], r_r.at[s], b, s).wait_recv()

    outs = res_out.shape[1]
    every = jnp.concatenate([unfold(rrx[j]) for j in range(nc)], axis=0)
    gt = (
        dot(every, kbuf[...].reshape(nc * rows, cdev), 0, 0) * sb_row
    )

    for j in range(nb):
        gsend[j] = gt[:, j * piece : (j + 1) * piece]

    def b_scatter(k, src, dst, ssem, rsem):
        d = lax.rem(b + k, nb)
        return copy(src.at[d], dst.at[b], ssem.at[k], rsem.at[b], d, c)

    def b_gather(k, src, dst, ssem, rsem):
        d = lax.rem(b + k, nb)
        return copy(src, dst.at[b], ssem.at[k], rsem.at[b], d, c)

    def b_wait(k, src, dst, ssem, rsem):
        d = lax.rem(b + k, nb)
        copy(src, dst.at[d], ssem.at[k], rsem.at[d], d, c).wait_recv()

    for k in range(1, nb):
        b_scatter(k, gsend, grx, g_s, g_r).start()
    grx[b] = gsend[b]

    def add_group(j):
        g = lax.rem(b - j + nb, nb) * nc

        @pl.loop(1 if j == 0 else 0, nc)
        def _(i):
            s = g + lax.rem(c - i + nc, nc)
            copy(offsend.at[0], offrx.at[s], o_s.at[i], o_r.at[s], b, c).wait_recv()
            copy(packed.at[0, pl.ds(0, slots)], eigrx.at[s], e_s.at[i], e_r.at[s], b, c).wait_recv()

        mark = offrx[g]
        for i in range(1, nc):
            mark = mark + offrx[g + i]
        sel = (
            lax.broadcasted_iota(jnp.int32, (cdev, nc * slots), 0) + 1 == mark.astype(jnp.int32)
        ).astype(jnp.float32).astype(jnp.bfloat16)
        part = pick(sel, eigrx[pl.ds(g, nc)].reshape(nc * slots, qb))
        ebar[...] = part if j == 0 else ebar[...] + part

    early = min(EARLY, nb)
    for j in range(early):
        add_group(j)

    for k in range(1, nb):
        b_wait(k, gown, grx, g_s, g_r)
    gsum = grx[0]
    for j in range(1, nb):
        gsum = gsum + grx[j]
    gown[...] = gsum
    gall[b] = gsum
    for k in range(1, nb):
        b_gather(k, gown, gall, ga_s, ga_r).start()
    for j in range(early, nb):
        add_group(j)
    for k in range(1, nb):
        b_wait(k, gown, gall, ga_s, ga_r)

    coeff = None
    for j in range(nb):
        part = dot(gall[j], ebar[j * piece : (j + 1) * piece], 1, 0)
        coeff = part if coeff is None else coeff + part
    og = outs // nc
    for j in range(nc):
        csend[j] = coeff[j * og : (j + 1) * og]

    def c_copy(k):
        d = lax.rem(c + k, nc)
        return copy(csend.at[d], crx.at[c], c_s.at[k], c_r.at[c], b, d)

    @pl.loop(1, nc)
    def _(k):
        c_copy(k).start()

    crx[c] = csend[c]

    @pl.loop(1, nc)
    def _(k):
        s = lax.rem(c - k + nc, nc)
        copy(csend.at[0], crx.at[s], c_s.at[k], c_r.at[s], b, s).wait_recv()

    csum = crx[0]
    for j in range(1, nc):
        csum = csum + crx[j]
    csum = csum * scale[b]
    cown[...] = csum
    call[c] = csum

    def ca_copy(k):
        return copy(cown, call.at[c], ca_s.at[k], ca_r.at[c], b, lax.rem(c + k, nc))

    @pl.loop(1, nc)
    def _(k):
        ca_copy(k).start()

    @pl.loop(1, nc)
    def _(k):
        s = lax.rem(c - k + nc, nc)
        copy(cown, call.at[s], ca_s.at[k], ca_r.at[s], b, s).wait_recv()

    scaled = jnp.concatenate([call[j] for j in range(nc)], axis=0)
    for j in range(nb):
        usend[j] = dot(scaled, ebar[j * piece : (j + 1) * piece], 1, 1)
    for k in range(1, nb):
        b_scatter(k, usend, urx, u_s, u_r).start()
    urx[b] = usend[b]
    for k in range(1, nb):
        b_wait(k, uown, urx, u_s, u_r)
    usum = urx[0]
    for j in range(1, nb):
        usum = usum + urx[j]
    usum = usum - gown[...]
    uown[...] = usum
    uall[b] = usum
    for k in range(1, nb):
        b_gather(k, uown, uall, ua_s, ua_r).start()
    for k in range(1, nb):
        b_wait(k, uown, uall, ua_s, ua_r)
    for j in range(nb):
        upd_out[:, j * piece : (j + 1) * piece] = uall[j]

    @pl.loop(1, nc)
    def _(k):
        f_copy(k).wait_send()
        p_copy(k).wait_send()
        r_copy(k).wait_send()
        c_copy(k).wait_send()
        ca_copy(k).wait_send()

    @pl.loop(1, n)
    def _(k):
        e_copy(k).wait_send()
        o_copy(k).wait_send()

    for k in range(1, nb):
        b_scatter(k, gsend, grx, g_s, g_r).wait_send()
        b_gather(k, gown, gall, ga_s, ga_r).wait_send()
        b_scatter(k, usend, urx, u_s, u_r).wait_send()
        b_gather(k, uown, uall, ua_s, ua_r).wait_send()


def per_device(
    pool_features,
    pool_targets,
    batch_index,
    centers,
    weights,
    eig_vectors,
    eig_scale,
    nys_owner,
    nys_offset,
):
    nb, nc = lax.axis_size("batch"), lax.axis_size("centers")
    n = nb * nc
    rows, dim = batch_index.shape[0], pool_features.shape[1]
    outs = pool_targets.shape[1]
    cdev = centers.shape[0]
    pts, q = eig_vectors.shape
    slots = max(2, 2 * pts // nc)
    qb, piece, og = q // nb, cdev // nb, outs // nc
    f32 = jnp.float32
    vm = pltpu.VMEM
    dma = pltpu.SemaphoreType.DMA
    spec = pl.BlockSpec(memory_space=pltpu.VMEM)
    pair = [dma((nc,)), dma((nc,))]
    every = [dma((n,)), dma((n,))]
    quad = [dma((nb,)), dma((nb,))]
    residual, update = pl.pallas_call(
        functools.partial(body, nb, nc),
        out_shape=(
            jax.ShapeDtypeStruct((rows, outs), f32),
            jax.ShapeDtypeStruct((outs, cdev), f32),
        ),
        in_specs=[spec] * 9,
        out_specs=(spec, spec),
        scratch_shapes=[
            vm((rows, dim), f32),
            vm((nc, rows, dim), f32),
            vm((nc, rows, cdev), f32),
            vm((nc, rows // 2, 2 * outs), f32),
            vm((nc, rows // 2, 2 * outs), f32),
            vm((rows // 2, 2 * outs), f32),
            vm((nc, rows // 2, 2 * outs), f32),
            vm((nb, nc * slots, qb), f32),
            vm((n, slots, qb), f32),
            vm((nc, 1, nc * slots), f32),
            vm((n, 1, nc * slots), f32),
            vm((cdev, qb), f32),
            vm((nb, outs, piece), f32),
            vm((nb, outs, piece), f32),
            vm((outs, piece), f32),
            vm((nb, outs, piece), f32),
            vm((nc, og, qb), f32),
            vm((nc, og, qb), f32),
            vm((og, qb), f32),
            vm((nc, og, qb), f32),
            vm((nb, outs, piece), f32),
            vm((nb, outs, piece), f32),
            vm((outs, piece), f32),
            vm((nb, outs, piece), f32),
        ]
        + pair * 3
        + every * 2
        + quad * 2
        + pair * 2
        + quad * 2,
        compiler_params=pltpu.CompilerParams(collective_id=0, has_side_effects=True),
    )(
        pool_features,
        pool_targets.T,
        batch_index[None, :],
        centers,
        weights.T,
        eig_vectors,
        eig_scale.reshape(nb, 1, qb),
        nys_owner.reshape(1, pts),
        nys_offset[None, :],
    )
    return (residual, update.T)


def solution(mesh):
    placed = (
        P(("batch", "centers"), None),
        P(("batch", "centers"), None),
        P(("batch", "centers")),
        P("centers", None),
        P("centers", None),
        P(("batch", "centers"), None),
        P(),
        P(("batch", "centers"), None),
        P(("batch", "centers")),
    )
    return jax.shard_map(
        per_device,
        mesh=mesh,
        in_specs=placed,
        out_specs=(P(("batch", "centers"), None), P("centers", None)),
        check_vma=False,
    )
```

profile of v0, /device:TPU:0, one launch (start us, length us, event | category | flops | bytes accessed | tf_op | source)
XLA Modules:
  0.0 68.9 jit_solution(18193320363769937373)
XLA Ops:
  0.6 65.3 %shard_map.104 = (f32[64,64]{1,0:T(8,128)}, f32[64,512]{1,0:T(8,128)}) custom-call(f32[1024,128]{1,0:T(8,128)} %pool_f.1, f32[64,1024]{1,0:T(8,128)} %bitcast.7, s32[1,64]{1,0:T(1,128)} %bitcast.11, f32[512,128]{1,0:T(8,128)} %cen.1, f32[64,512]{1,0:T(8,128)} %bitcast.9, f32[128,1024]{1,0:T(8,128)} %eig.1, f32[4,1,256]{2,1,0:T(1,128)} %bitcast.10, ...), custom_call_target="tpu_custom_call" | custom-call | tf_op jit(solution)/shard_map/pallas_call | solution.py:476
  65.9 1.4 %copy.13 = f32[64,64]{1,0:T(8,128)} copy(f32[64,64]{1,0:T(8,128)} %get-tuple-element.8) | data formatting | bytes 32768
  67.3 1.6 %copy.14 = f32[512,64]{0,1:T(8,128)} copy(f32[512,64]{0,1:T(8,128)} %bitcast.8) | data formatting | bytes 262144
where the time goes:
time: 69.1 us; the launch traced here: 68.9 us
  Pallas kernels  65.3 us (95%)
  local copies, waits for them, and re-layouts  2.94 us (4%)
    pallas_call x1, Pallas kernels, per_device(): pl.pallas_call(functools.partial(body, nb, nc), out_shape=(jax.ShapeDtype...  65.3 us
    unnamed x2, local copies, waits for them, and re-layouts  2.94 us

commit v1 on v0

v1 whole, which is shorter than its diff:
```python
import functools
import math

import jax
import jax.numpy as jnp
from jax import lax
from jax.experimental import pallas as pl
from jax.experimental.pallas import tpu as pltpu
from jax.sharding import PartitionSpec as P

DEPTH = 3
EPS = 1e-06
HIGH = lax.Precision.HIGHEST
MESH = pl.DeviceIdType.MESH
LOW = jnp.bfloat16
F32 = jnp.float32
FAR = (2, 1, 1, 1, 0)
NEAR = (0, 2, 2, 2, 2)
ACOS = (
    1.5707963050,
    -0.2145988016,
    0.0889789874,
    -0.0501743046,
    0.0308918810,
    -0.0170881256,
    0.0066700901,
    -0.0012624911,
)


def dot(a, b, ca, cb):
    return lax.dot_general(a, b, (((ca,), (cb,)), ((), ())), preferred_element_type=F32)


def exact(a, b, ca, cb):
    return lax.dot_general(
        a, b, (((ca,), (cb,)), ((), ())), precision=HIGH, preferred_element_type=F32
    )


def split(x):
    hi = x.astype(LOW)
    return hi, (x - hi.astype(F32)).astype(LOW)


def dot3(a, b, ca, cb):
    (ah, al), (bh, bl) = a, b
    rows = ah.shape[1 - ca]
    both = dot(jnp.concatenate([ah, al], axis=1 - ca), bh, ca, cb)
    return both[:rows] + both[rows:] + dot(ah, bl, ca, cb)


def fold(x):
    h = x.shape[0] // 2
    return jnp.concatenate([x[:h], x[h:]], axis=1)


def unfold(x):
    h = x.shape[1] // 2
    return jnp.concatenate([x[:, :h], x[:, h:]], axis=0)


def arc_parts(x):
    u = jnp.maximum(1.0 - x, 1e-30)
    poly = jnp.full_like(x, ACOS[-1] / math.pi)
    for a in ACOS[-2::-1]:
        poly = poly * x + a / math.pi
    v = u * (1.0 + x)
    return u * lax.rsqrt(u) * poly, v * lax.rsqrt(v) * (1.0 / math.pi)


def tangent_kernel(cosine):
    arc, sine = arc_parts(jnp.abs(cosine))
    remain = jnp.where(cosine < 0.0, arc, 1.0 - arc)
    prod = remain * cosine
    sigma = sine + prod
    tangent = sigma + prod
    for _ in range(DEPTH - 1):
        arc, sine = arc_parts(sigma)
        remain = 1.0 - arc
        sigma = sine + remain * sigma
        tangent = sigma + tangent * remain
    return tangent


def body(
    nb,
    nc,
    pool_f_h,
    pool_t_h,
    index_h,
    cen_h,
    wts_h,
    eig_h,
    scale_h,
    owner_h,
    offset_h,
    res_out,
    upd_out,
    pool_f,
    pool_t,
    index,
    index_s,
    cen,
    wts,
    eig,
    scale,
    owner,
    offset,
    res_v,
    upd_v,
    feat,
    feat_all,
    ccat,
    wcat,
    kh,
    kl,
    ppart,
    prx,
    rsend,
    rrx,
    packed,
    eigrx,
    offsend,
    offrx,
    ebar,
    gsend,
    grx,
    gown,
    gxrx,
    gall,
    csend,
    crx,
    cown,
    call,
    usend,
    urx,
    uown,
    uxrx,
    uall,
    in_s,
    out_s,
    f_s,
    f_r,
    p_s,
    p_r,
    r_s,
    r_r,
    e_s,
    e_r,
    o_s,
    o_r,
    g_s,
    g_r,
    c_s,
    c_r,
    ca_s,
    ca_r,
    u_s,
    u_r,
):
    b = lax.axis_index("batch")
    c = lax.axis_index("centers")
    n = nb * nc
    me = b * nc + c
    half = nb // 2
    k2, x = lax.rem(b, 2), lax.div(b, 2)
    z, y = lax.div(c, 2), lax.rem(c, 2)
    nz = nc // 2
    mine = c * nb + b
    rows, dim = feat.shape
    outs, cdev = wts.shape
    pts = owner.shape[1]
    group = 2 * nb
    slots = packed.shape[1] // nc
    qb = packed.shape[2]
    piece = cdev // 4
    rows_total = rows * n

    def copy(src, dst, ssem, rsem, db, dc):
        return pltpu.make_async_remote_copy(
            src_ref=src,
            dst_ref=dst,
            send_sem=ssem,
            recv_sem=rsem,
            device_id=(db, dc),
            device_id_type=MESH,
        )

    barrier = pltpu.get_barrier_semaphore()

    @pl.loop(1, n)
    def _(k):
        d = lax.rem(me + k, n)
        pl.semaphore_signal(
            barrier, inc=1, device_id=(lax.div(d, nc), lax.rem(d, nc)), device_id_type=MESH
        )

    loads = [
        pltpu.make_async_copy(src, dst, in_s.at[i])
        for i, (src, dst) in enumerate(
            (
                (index_h, index_s),
                (pool_f_h, pool_f),
                (owner_h, owner),
                (offset_h, offset),
                (eig_h, eig),
                (cen_h, cen),
                (wts_h, wts),
                (scale_h, scale),
                (index_h, index),
                (pool_t_h, pool_t),
            )
        )
    ]
    for load in loads:
        load.start()

    loads[0].wait()
    loads[1].wait()

    @pl.loop(0, rows, unroll=8)
    def _(j):
        feat[pl.ds(j, 1), :] = pool_f[pl.ds(index_s[0, j], 1), :]

    feat_all[c] = feat[...]

    loads[2].wait()
    loads[3].wait()
    own = owner[...]
    hot = (own == lax.broadcasted_iota(jnp.int32, (nc, pts), 0)).astype(F32)
    upper = (
        lax.broadcasted_iota(jnp.int32, (pts, pts), 0)
        < lax.broadcasted_iota(jnp.int32, (pts, pts), 1)
    ).astype(F32)
    rank = jnp.sum(
        dot(hot.astype(LOW), upper.astype(LOW), 1, 0) * hot, axis=0, keepdims=True
    ).astype(jnp.int32)
    place = (
        (lax.broadcasted_iota(jnp.int32, (nc * slots, pts), 0) == own * slots + rank)
        .astype(F32)
        .astype(LOW)
    )
    loads[4].wait()
    both = jnp.concatenate(split(eig[...]), axis=0)
    place2 = jnp.concatenate([place, place], axis=1)
    for j in range(nb):
        packed[j] = dot(place2, both[:, j * qb : (j + 1) * qb], 1, 0)
    here = (
        lax.broadcasted_iota(jnp.int32, (group * slots, pts), 0)
        == (y * nb + b) * slots + rank
    ).astype(F32)
    marks = exact(hot * (offset[...].astype(F32) + 1.0), here, 1, 1)
    for j in range(nc):
        offsend[j] = marks[j : j + 1]
    eigrx[mine] = packed[b, pl.ds(pl.multiple_of(c * slots, slots), slots)]
    offrx[mine] = offsend[c]

    loads[5].wait()
    cval = cen[...]
    csq = cval * cval
    ncol = jnp.mean(csq, axis=1, keepdims=True) + EPS
    ch, cl = split(cval / (jnp.sqrt(ncol) * dim))
    ccat[...] = jnp.concatenate([ch, cl, ch, cl], axis=1)
    sb_row = jnp.sqrt(exact(jnp.full((8, dim), 1.0 / dim, F32), csq, 1, 1)[0:1] + EPS)
    loads[6].wait()
    wcat[...] = jnp.concatenate(split(wts[...] * sb_row), axis=0)

    pl.semaphore_wait(barrier, n - 1)

    def at(zo, yo):
        return (z ^ zo) * 2 + (y ^ yo)

    def f_copy(t):
        d = at(lax.div(t, 2), lax.rem(t, 2))
        return copy(feat, feat_all.at[c], f_s.at[t], f_r.at[c], b, d)

    def f_wait(t):
        s = at(lax.div(t, 2), lax.rem(t, 2))
        copy(feat, feat_all.at[s], f_s.at[t], f_r.at[s], b, s).wait_recv()

    @pl.loop(1, nc)
    def _(t):
        f_copy(nc - t).start()

    def e_place(t):
        o = n - 1 - t
        return lax.rem(b + lax.rem(o, nb), nb), at(lax.div(o, group), lax.rem(lax.div(o, nb), 2))

    def e_source(o):
        return lax.rem(b - lax.rem(o, nb) + nb, nb), at(
            lax.div(o, group), lax.rem(lax.div(o, nb), 2)
        )

    def e_copy(t):
        db, dc = e_place(t)
        return copy(
            packed.at[db, pl.ds(pl.multiple_of(dc * slots, slots), slots)],
            eigrx.at[mine],
            e_s.at[t],
            e_r.at[mine],
            db,
            dc,
        )

    def o_copy(t):
        db, dc = e_place(t)
        return copy(offsend.at[dc], offrx.at[mine], o_s.at[t], o_r.at[mine], db, dc)

    marks_at = [0, n // 2]
    ends_at = [n // 2, n - 1]

    def e_start(step):
        for kind, plan in enumerate((FAR, NEAR)):
            lo, total = marks_at[kind], ends_at[kind]
            hi = total if step == len(plan) - 1 else min(total, lo + plan[step] * n // 16)
            marks_at[kind] = hi

            @pl.loop(lo, hi)
            def _(t):
                e_copy(t).start()

    e_start(0)

    def p_copy(t):
        s = at(lax.div(t, 2), lax.rem(t, 2))
        return copy(ppart.at[s], prx.at[c], p_s.at[t], p_r.at[c], b, s)

    def pair(p):
        zs = z ^ p
        av = feat_all[pl.ds(zs * 2, 2)].reshape(2 * rows, dim)
        na = jnp.mean(av * av, axis=1, keepdims=True) + EPS
        ah, al = split(av * lax.rsqrt(na))
        k = tangent_kernel(dot(jnp.concatenate([ah, ah, al, al], axis=1), ccat[...], 1, 1))
        hi, lo = split(k)
        kh[zs] = hi
        kl[zs] = lo
        top = dot(hi, wcat[...], 1, 1)
        pred = top[:, :outs] + top[:, outs:] + dot(lo, wcat[:outs], 1, 1)
        return fold(pred[:rows]), fold(pred[rows:])

    f_wait(1)
    low, high = pair(0)
    prx[c] = jnp.where(y == 0, low, high)
    ppart[c ^ 1] = jnp.where(y == 0, high, low)
    p_copy(1).start()
    e_start(1)

    def later(p):
        f_wait(2 * p)
        f_wait(2 * p + 1)
        lo, hi = pair(p)
        zs = (z ^ p) * 2
        ppart[zs] = lo
        ppart[zs + 1] = hi
        p_copy(2 * p).start()
        p_copy(2 * p + 1).start()

    for p in range(1, 3):
        later(p)
        e_start(p + 1)

    @pl.loop(3, nz)
    def _(p):
        later(p)

    a = feat[...]
    sa = jnp.sqrt(jnp.mean(a * a, axis=1, keepdims=True) + EPS)
    loads[7].wait()
    loads[8].wait()
    loads[9].wait()
    drawn = (
        (lax.broadcasted_iota(jnp.int32, (pool_t.shape[1], rows), 0) == index[...])
        .astype(F32)
        .astype(LOW)
    )
    th, tl = split(pool_t[...])
    picked = dot(jnp.concatenate([th, tl], axis=0), drawn, 1, 0)
    targ = (picked[:outs] + picked[outs:]).T

    @pl.loop(1, nc)
    def _(t):
        s = at(lax.div(t, 2), lax.rem(t, 2))
        copy(ppart.at[s], prx.at[s], p_s.at[t], p_r.at[s], b, s).wait_recv()

    pred = prx[0]
    for j in range(1, nc):
        pred = pred + prx[j]
    resid = unfold(pred) * sa - targ
    folded = fold(resid * (sa / math.sqrt(rows_total)))
    rsend[...] = folded
    rrx[c] = folded

    def r_copy(t):
        return copy(
            rsend, rrx.at[c], r_s.at[t], r_r.at[c], b, at(lax.div(t, 2), lax.rem(t, 2))
        )

    @pl.loop(1, nc)
    def _(t):
        r_copy(nc - t).start()

    @pl.loop(0, n - 1)
    def _(t):
        o_copy(t).start()

    e_start(4)

    res_v[...] = resid
    res_store = pltpu.make_async_copy(res_v, res_out, out_s.at[0])
    res_store.start()

    @pl.loop(1, nc)
    def _(t):
        s = at(lax.div(t, 2), lax.rem(t, 2))
        copy(rsend, rrx.at[s], r_s.at[t], r_r.at[s], b, s).wait_recv()

    every = jnp.concatenate([unfold(rrx[j]) for j in range(nc)], axis=0)
    eh, el = split(every)
    khv = kh[...].reshape(nc * rows, cdev)
    up = dot(jnp.concatenate([eh, el], axis=1), khv, 0, 0)
    gt = (
        up[:outs] + up[outs:] + dot(eh, kl[...].reshape(nc * rows, cdev), 0, 0)
    ) * sb_row

    def reduce_parts(part, send, rx, owned, xrx, full, ssem, rsem):
        mate = b + 1 - 2 * k2
        started = []
        for j in range(4):
            send[j] = part[:, j * piece : (j + 1) * piece]
        away = copy(
            send.at[pl.ds(2 * (1 - k2), 2)], rx, ssem.at[0], rsem.at[0], mate, c
        )
        away.start()
        started.append(away)
        yield
        away.wait_recv()
        owned[...] = send[pl.ds(2 * k2, 2)] + rx[...]
        for i in range(1, half):
            d = lax.rem(x + i, half) * 2 + k2
            out = copy(owned, xrx.at[x], ssem.at[i], rsem.at[1 + x], d, c)
            out.start()
            started.append(out)
        yield
        total = owned[...]
        for i in range(1, half):
            s = lax.rem(x + i, half)
            copy(owned, xrx.at[s], ssem.at[i], rsem.at[1 + s], s * 2 + k2, c).wait_recv()
            total = total + xrx[s]
        full[pl.ds(2 * k2, 2)] = total
        across = copy(
            full.at[pl.ds(2 * k2, 2)],
            full.at[pl.ds(2 * k2, 2)],
            ssem.at[half],
            rsem.at[1 + half],
            mate,
            c,
        )
        across.start()
        started.append(across)
        yield
        copy(
            full.at[pl.ds(2 * k2, 2)],
            full.at[pl.ds(2 * (1 - k2), 2)],
            ssem.at[half],
            rsem.at[1 + half],
            mate,
            c,
        ).wait_recv()
        yield
        for s in started:
            s.wait_send()
        yield

    def add_group(p):
        zs = z ^ p
        base = zs * group

        @pl.loop(1 if p == 0 else 0, group)
        def _(i):
            sb, sc = e_source(p * group + i)
            s = sc * nb + sb
            t = n - 1 - (p * group + i)
            copy(offsend.at[0], offrx.at[s], o_s.at[t], o_r.at[s], b, c).wait_recv()
            copy(packed.at[0, pl.ds(0, slots)], eigrx.at[s], e_s.at[t], e_r.at[s], b, c).wait_recv()

        mark = offrx[base]
        for i in range(1, group):
            mark = mark + offrx[base + i]
        sel = (
            (
                lax.broadcasted_iota(jnp.int32, (cdev, group * slots), 0) + 1
                == mark.astype(jnp.int32)
            )
            .astype(F32)
            .astype(LOW)
        )
        parts = split(eigrx[pl.ds(base, group)].reshape(group * slots, qb))
        return dot(
            jnp.concatenate([sel, sel], axis=1), jnp.concatenate(parts, axis=0), 1, 0
        )

    g_sum = reduce_parts(gt, gsend, grx, gown, gxrx, gall, g_s, g_r)
    next(g_sum)
    next(g_sum)
    ebar[...] = add_group(0)
    next(g_sum)
    ebar[...] += add_group(1)
    next(g_sum)

    def add_later(p):
        ebar[...] += add_group(p)

    for p in range(2, min(nz, 4)):
        add_later(p)
    for p in range(4, nz):
        add_later(p)

    g = jnp.concatenate([gall[j] for j in range(4)], axis=1)
    ebh, ebl = split(ebar[...])
    coeff = dot3(split(g), (ebh, ebl), 1, 0)
    og = outs // nc
    for j in range(nc):
        csend[j] = coeff[j * og : (j + 1) * og]

    def c_copy(t):
        d = at(lax.div(t, 2), lax.rem(t, 2))
        return copy(csend.at[d], crx.at[c], c_s.at[t], c_r.at[c], b, d)

    @pl.loop(1, nc)
    def _(t):
        c_copy(nc - t).start()

    crx[c] = csend[c]

    @pl.loop(1, nc)
    def _(t):
        s = at(lax.div(t, 2), lax.rem(t, 2))
        copy(csend.at[0], crx.at[s], c_s.at[t], c_r.at[s], b, s).wait_recv()

    csum = crx[0]
    for j in range(1, nc):
        csum = csum + crx[j]
    csum = csum * scale[b]
    cown[...] = csum
    call[c] = csum

    def ca_copy(t):
        return copy(
            cown, call.at[c], ca_s.at[t], ca_r.at[c], b, at(lax.div(t, 2), lax.rem(t, 2))
        )

    @pl.loop(1, nc)
    def _(t):
        ca_copy(nc - t).start()

    @pl.loop(1, nc)
    def _(t):
        s = at(lax.div(t, 2), lax.rem(t, 2))
        copy(cown, call.at[s], ca_s.at[t], ca_r.at[s], b, s).wait_recv()

    scaled = jnp.concatenate([call[j] for j in range(nc)], axis=0)
    u = dot3(split(scaled), (ebh, ebl), 1, 1)
    u_sum = reduce_parts(u, usend, urx, uown, uxrx, uall, u_s, u_r)
    for _ in range(4):
        next(u_sum)
    for j in range(4):
        upd_v[:, j * piece : (j + 1) * piece] = uall[j] - gall[j]
    upd_store = pltpu.make_async_copy(upd_v, upd_out, out_s.at[1])
    upd_store.start()

    @pl.loop(1, nc)
    def _(t):
        f_copy(t).wait_send()
        p_copy(t).wait_send()
        r_copy(t).wait_send()
        c_copy(t).wait_send()
        ca_copy(t).wait_send()

    @pl.loop(0, n - 1)
    def _(t):
        e_copy(t).wait_send()
        o_copy(t).wait_send()

    next(g_sum)
    next(u_sum)
    res_store.wait()
    upd_store.wait()


def per_device(
    pool_features,
    pool_targets,
    batch_index,
    centers,
    weights,
    eig_vectors,
    eig_scale,
    nys_owner,
    nys_offset,
):
    nb, nc = lax.axis_size("batch"), lax.axis_size("centers")
    n = nb * nc
    rows, (pool, dim) = batch_index.shape[0], pool_features.shape
    outs = pool_targets.shape[1]
    cdev = centers.shape[0]
    pts, q = eig_vectors.shape
    slots = max(2, 2 * pts // nc)
    group, half = 2 * nb, nb // 2
    qb, piece, og = q // nb, cdev // 4, outs // nc
    vm = pltpu.VMEM
    dma = pltpu.SemaphoreType.DMA
    spec = pl.BlockSpec(memory_space=pl.ANY)
    pair = [dma((nc,)), dma((nc,))]
    every = [dma((n,)), dma((n,))]
    sums = [dma((half + 1,)), dma((half + 2,))]
    reduced = [
        vm((4, outs, piece), F32),
        vm((2, outs, piece), F32),
        vm((2, outs, piece), F32),
        vm((half, 2, outs, piece), F32),
        vm((4, outs, piece), F32),
    ]
    residual, update = pl.pallas_call(
        functools.partial(body, nb, nc),
        out_shape=(
            jax.ShapeDtypeStruct((rows, outs), F32),
            jax.ShapeDtypeStruct((outs, cdev), F32),
        ),
        in_specs=[spec] * 9,
        out_specs=(spec, spec),
        scratch_shapes=[
            vm((pool, dim), F32),
            vm((outs, pool), F32),
            vm((1, rows), jnp.int32),
            pltpu.SMEM((1, rows), jnp.int32),
            vm((cdev, dim), F32),
            vm((outs, cdev), F32),
            vm((pts, q), F32),
            vm((nb, 1, qb), F32),
            vm((1, pts), jnp.int32),
            vm((1, pts), jnp.int32),
            vm((rows, outs), F32),
            vm((outs, cdev), F32),
            vm((rows, dim), F32),
            vm((nc, rows, dim), F32),
            vm((cdev, 4 * dim), LOW),
            vm((2 * outs, cdev), LOW),
            vm((nc // 2, 2 * rows, cdev), LOW),
            vm((nc // 2, 2 * rows, cdev), LOW),
            vm((nc, rows // 2, 2 * outs), F32),
            vm((nc, rows // 2, 2 * outs), F32),
            vm((rows // 2, 2 * outs), F32),
            vm((nc, rows // 2, 2 * outs), F32),
            vm((nb, nc * slots, qb), F32),
            vm((n, slots, qb), F32),
            vm((nc, 1, group * slots), F32),
            vm((n, 1, group * slots), F32),
            vm((cdev, qb), F32),
        ]
        + reduced
        + [
            vm((nc, og, qb), F32),
            vm((nc, og, qb), F32),
            vm((og, qb), F32),
            vm((nc, og, qb), F32),
        ]
        + reduced
        + [dma((10,)), dma((2,))]
        + pair * 3
        + every * 2
        + sums
        + pair * 2
        + sums,
        compiler_params=pltpu.CompilerParams(collective_id=0, has_side_effects=True),
    )(
        pool_features,
        pool_targets.T,
        batch_index[None, :],
        centers,
        weights.T,
        eig_vectors,
        eig_scale.reshape(nb, 1, qb),
        nys_owner.reshape(1, pts),
        nys_offset[None, :],
    )
    return (residual, update.T)


def solution(mesh):
    placed = (
        P(("batch", "centers"), None),
        P(("batch", "centers"), None),
        P(("batch", "centers")),
        P("centers", None),
        P("centers", None),
        P(("batch", "centers"), None),
        P(),
        P(("batch", "centers"), None),
        P(("batch", "centers")),
    )
    return jax.shard_map(
        per_device,
        mesh=mesh,
        in_specs=placed,
        out_specs=(P(("batch", "centers"), None), P("centers", None)),
        check_vma=False,
    )
```

time: 69.1 us -> 67.1 us (0.971)
  Pallas kernels: 65.3 us -> 63.3 us
    pallas_call x1, Pallas kernels: 65.3 us -> 63.3 us  [per_device(): pl.pallas_call(functools.partial(body, nb, nc), out_shape=(jax.ShapeDtype...]
where the time goes in v1:
time: 67.1 us; the launch traced here: 66.9 us
  Pallas kernels  63.3 us (94%)
  local copies, waits for them, and re-layouts  2.94 us (4%)
    pallas_call x1, Pallas kernels, per_device(): pl.pallas_call(functools.partial(body, nb, nc), out_shape=(jax.ShapeDtype...  63.3 us
    unnamed x2, local copies, waits for them, and re-layouts  2.94 us

profile of v1, /device:TPU:0, one launch (start us, length us, event | category | flops | bytes accessed | tf_op | source)
XLA Modules:
  0.0 66.9 jit_solution(16685567410515057517)
XLA Ops:
  0.6 63.3 %shard_map.104 = (f32[64,64]{1,0:T(8,128)}, f32[64,512]{1,0:T(8,128)}) custom-call(f32[1024,128]{1,0:T(8,128)} %pool_f_h.1, f32[64,1024]{1,0:T(8,128)} %bitcast.7, s32[1,64]{1,0:T(1,128)} %bitcast.11, f32[512,128]{1,0:T(8,128)} %cen_h.1, f32[64,512]{1,0:T(8,128)} %bitcast.9, f32[128,1024]{1,0:T(8,128)} %eig_h.1, f32[4,1,256]{2,1,0:T(1,128)} %bitcast.10, ...), custom_call_target="tpu_custom_call" | custom-call | tf_op jit(solution)/shard_map/pallas_call | solution.py:624
  64.0 1.4 %copy.13 = f32[64,64]{1,0:T(8,128)} copy(f32[64,64]{1,0:T(8,128)} %get-tuple-element.8) | data formatting | bytes 32768
  65.3 1.6 %copy.14 = f32[512,64]{0,1:T(8,128)} copy(f32[512,64]{0,1:T(8,128)} %bitcast.8) | data formatting | bytes 262144

commit v2 on v1

--- a/solution.py
+++ b/solution.py
@@ -11,11 +11,12 @@
 DEPTH = 3
 EPS = 1e-06
 HIGH = lax.Precision.HIGHEST
+VMEM = 32 * 2**20
 MESH = pl.DeviceIdType.MESH
 LOW = jnp.bfloat16
 F32 = jnp.float32
-FAR = (2, 1, 1, 1, 0)
-NEAR = (0, 2, 2, 2, 2)
+FAR = (8, 0, 0, 0, 0, 16)
+NEAR = (7, 0, 0, 0, 0, 16)
 ACOS = (
     1.5707963050,
     -0.2145988016,
@@ -140,6 +141,7 @@
     uall,
     in_s,
     out_s,
+    told,
     f_s,
     f_r,
     p_s,
@@ -189,12 +191,26 @@
 
     barrier = pltpu.get_barrier_semaphore()
 
-    @pl.loop(1, n)
-    def _(k):
-        d = lax.rem(me + k, n)
-        pl.semaphore_signal(
-            barrier, inc=1, device_id=(lax.div(d, nc), lax.rem(d, nc)), device_id_type=MESH
-        )
+    def greet(zd, first):
+        @pl.loop(first, group)
+        def _(i):
+            o = lax.rem(b + (y * nb) + i, group)
+            pl.semaphore_signal(
+                barrier,
+                inc=1,
+                device_id=(lax.rem(o, nb), zd * 2 + lax.div(o, nb)),
+                device_id_type=MESH,
+            )
+
+    greet(z, 1)
+
+    @pl.when(z > 0)
+    def _():
+        greet(z - 1, 0)
+
+    @pl.when(z < nz - 1)
+    def _():
+        greet(z + 1, 0)
 
     loads = [
         pltpu.make_async_copy(src, dst, in_s.at[i])
@@ -224,6 +240,93 @@
         feat[pl.ds(j, 1), :] = pool_f[pl.ds(index_s[0, j], 1), :]
 
     feat_all[c] = feat[...]
+
+    inner = jnp.logical_and(z > 0, z < nz - 1)
+
+    @pl.when(inner)
+    def _():
+        pl.semaphore_wait(barrier, 3 * group - 1)
+
+    @pl.when(jnp.logical_not(inner))
+    def _():
+        pl.semaphore_wait(barrier, 2 * group - 1)
+
+    def at(zo, yo):
+        return (z ^ zo) * 2 + (y ^ yo)
+
+    mate = at(0, 1)
+
+    def spread(src, dst, ssem, rsem, t):
+        p, on = lax.div(t, 2), lax.rem(t, 2)
+        s = at(p * on, 0)
+        d = at(p * (1 - on), on)
+        return copy(src if src is not None else dst.at[s], dst.at[s], ssem.at[t], rsem.at[s], b, d)
+
+    def spread_pass(dst, ssem, rsem, p):
+        s = at(p, 0)
+        copy(dst.at[s], dst.at[s], ssem.at[0], rsem.at[s], b, s).wait_recv()
+        spread(None, dst, ssem, rsem, 2 * p + 1).start()
+
+    def spread_end(dst, ssem, rsem, p):
+        s = at(p, 1)
+        copy(dst.at[s], dst.at[s], ssem.at[0], rsem.at[s], b, s).wait_recv()
+
+    def spread_sent(src, dst, ssem, rsem):
+        spread(src, dst, ssem, rsem, 1).wait_send()
+
+        @pl.loop(2, nc)
+        def _(t):
+            spread(None, dst, ssem, rsem, t).wait_send()
+
+    def tell(which, zd):
+        pl.semaphore_signal(
+            told.at[which], inc=1, device_id=(b, zd * 2 + y), device_id_type=MESH
+        )
+
+    @pl.when(z == 1)
+    def _():
+        tell(0, z + 1)
+
+    @pl.when(z == nz - 2)
+    def _():
+        tell(1, z - 1)
+
+    @pl.loop(1, nz)
+    def _(p):
+        @pl.when(jnp.abs((z ^ p) - z) == 1)
+        def _():
+            spread(feat, feat_all, f_s, f_r, 2 * p).start()
+
+    spread(feat, feat_all, f_s, f_r, 1).start()
+
+    def hear():
+        @pl.when(z >= 2)
+        def _():
+            pl.semaphore_wait(told.at[0], 1)
+
+            @pl.when(z < nz - 1)
+            def _():
+                tell(0, z + 1)
+
+        @pl.when(z <= nz - 3)
+        def _():
+            pl.semaphore_wait(told.at[1], 1)
+
+            @pl.when(z > 0)
+            def _():
+                tell(1, z - 1)
+
+        @pl.loop(1, nz)
+        def _(i):
+            p = nz - i
+
+            @pl.when(jnp.abs((z ^ p) - z) > 1)
+            def _():
+                spread(feat, feat_all, f_s, f_r, 2 * p).start()
+
+    @pl.when(z >= nz // 2)
+    def _():
+        hear()
 
     loads[2].wait()
     loads[3].wait()
@@ -266,22 +369,9 @@
     loads[6].wait()
     wcat[...] = jnp.concatenate(split(wts[...] * sb_row), axis=0)
 
-    pl.semaphore_wait(barrier, n - 1)
-
-    def at(zo, yo):
-        return (z ^ zo) * 2 + (y ^ yo)
-
-    def f_copy(t):
-        d = at(lax.div(t, 2), lax.rem(t, 2))
-        return copy(feat, feat_all.at[c], f_s.at[t], f_r.at[c], b, d)
-
-    def f_wait(t):
-        s = at(lax.div(t, 2), lax.rem(t, 2))
-        copy(feat, feat_all.at[s], f_s.at[t], f_r.at[s], b, s).wait_recv()
-
-    @pl.loop(1, nc)
-    def _(t):
-        f_copy(nc - t).start()
+    @pl.when(z < nz // 2)
+    def _():
+        hear()
 
     def e_place(t):
         o = n - 1 - t
@@ -313,7 +403,7 @@
     def e_start(step):
         for kind, plan in enumerate((FAR, NEAR)):
             lo, total = marks_at[kind], ends_at[kind]
-            hi = total if step == len(plan) - 1 else min(total, lo + plan[step] * n // 16)
+            hi = total if step == len(plan) - 1 else min(total, lo + plan[step] * n // 32)
             marks_at[kind] = hi
 
             @pl.loop(lo, hi)
@@ -339,7 +429,7 @@
         pred = top[:, :outs] + top[:, outs:] + dot(lo, wcat[:outs], 1, 1)
         return fold(pred[:rows]), fold(pred[rows:])
 
-    f_wait(1)
+    spread_end(feat_all, f_s, f_r, 0)
     low, high = pair(0)
     prx[c] = jnp.where(y == 0, low, high)
     ppart[c ^ 1] = jnp.where(y == 0, high, low)
@@ -347,8 +437,7 @@
     e_start(1)
 
     def later(p):
-        f_wait(2 * p)
-        f_wait(2 * p + 1)
+        spread_end(feat_all, f_s, f_r, p)
         lo, hi = pair(p)
         zs = (z ^ p) * 2
         ppart[zs] = lo
@@ -356,13 +445,21 @@
         p_copy(2 * p).start()
         p_copy(2 * p + 1).start()
 
-    for p in range(1, 3):
+    spread_pass(feat_all, f_s, f_r, 1)
+    spread_pass(feat_all, f_s, f_r, 2)
+    later(1)
+    e_start(2)
+    spread_pass(feat_all, f_s, f_r, 3)
+    later(2)
+    e_start(3)
+
+    @pl.loop(3, nz - 1)
+    def _(p):
+        spread_pass(feat_all, f_s, f_r, p + 1)
         later(p)
-        e_start(p + 1)
-
-    @pl.loop(3, nz)
-    def _(p):
-        later(p)
+
+    later(nz - 1)
+    e_start(4)
 
     a = feat[...]
     sa = jnp.sqrt(jnp.mean(a * a, axis=1, keepdims=True) + EPS)
@@ -404,7 +501,7 @@
     def _(t):
         o_copy(t).start()
 
-    e_start(4)
+    e_start(5)
 
     res_v[...] = resid
     res_store = pltpu.make_async_copy(res_v, res_out, out_s.at[0])
@@ -569,9 +666,10 @@
     upd_store = pltpu.make_async_copy(upd_v, upd_out, out_s.at[1])
     upd_store.start()
 
+    spread_sent(feat, feat_all, f_s, f_r)
+
     @pl.loop(1, nc)
     def _(t):
-        f_copy(t).wait_send()
         p_copy(t).wait_send()
         r_copy(t).wait_send()
         c_copy(t).wait_send()
@@ -627,7 +725,7 @@
             jax.ShapeDtypeStruct((rows, outs), F32),
             jax.ShapeDtypeStruct((outs, cdev), F32),
         ),
-        in_specs=[spec] * 9,
+        in_specs=[pl.BlockSpec(memory_space=pltpu.HBM)] * 9,
         out_specs=(spec, spec),
         scratch_shapes=[
             vm((pool, dim), F32),
@@ -666,23 +764,30 @@
             vm((nc, og, qb), F32),
         ]
         + reduced
-        + [dma((10,)), dma((2,))]
+        + [dma((10,)), dma((2,)), pltpu.SemaphoreType.REGULAR((2,))]
         + pair * 3
         + every * 2
         + sums
         + pair * 2
         + sums,
-        compiler_params=pltpu.CompilerParams(collective_id=0, has_side_effects=True),
+        compiler_params=pltpu.CompilerParams(
+            collective_id=0, has_side_effects=True, vmem_limit_bytes=VMEM
+        ),
     )(
-        pool_features,
-        pool_targets.T,
-        batch_index[None, :],
-        centers,
-        weights.T,
-        eig_vectors,
-        eig_scale.reshape(nb, 1, qb),
-        nys_owner.reshape(1, pts),
-        nys_offset[None, :],
+        *(
+            pltpu.with_memory_space_constraint(array, pltpu.HBM)
+            for array in (
+                pool_features,
+                pool_targets.T,
+                batch_index[None, :],
+                centers,
+                weights.T,
+                eig_vectors,
+                eig_scale.reshape(nb, 1, qb),
+                nys_owner.reshape(1, pts),
+                nys_offset[None, :],
+            )
+        )
     )
     return (residual, update.T)
 

time: 67.1 us -> 62 us (0.924)
  Pallas kernels: 63.3 us -> 59.9 us
  local copies, waits for them, and re-layouts: 2.94 us -> 1.27 us
    pallas_call x1, Pallas kernels: 63.3 us -> 59.9 us  [per_device(): pl.pallas_call(functools.partial(body, nb, nc), out_shape=(jax.ShapeDtype...]
    unnamed x2, local copies, waits for them, and re-layouts: 2.94 us -> 1.27 us
where the time goes in v2:
time: 62 us; the launch traced here: 61.8 us
  Pallas kernels  59.9 us (97%)
  local copies, waits for them, and re-layouts  1.27 us (2%)
  between operations  0.64 us (1%)
    pallas_call x1, Pallas kernels, per_device(): pl.pallas_call(functools.partial(body, nb, nc), out_shape=(jax.ShapeDtype...  59.9 us
    unnamed x2, local copies, waits for them, and re-layouts  1.27 us

profile of v2, /device:TPU:0, one launch (start us, length us, event | category | flops | bytes accessed | tf_op | source)
XLA Modules:
  0.0 61.8 jit_solution(6899802422204661768)
XLA Ops:
  0.6 59.9 %shard_map.104 = (f32[64,64]{1,0:T(8,128)S(1)}, f32[64,512]{1,0:T(8,128)S(1)}) custom-call(f32[1024,128]{1,0:T(8,128)} %pool_f_h.1, f32[64,1024]{1,0:T(8,128)} %bitcast.8, s32[1,64]{1,0:T(1,128)} %bitcast.11, f32[512,128]{1,0:T(8,128)} %cen_h.1, f32[64,512]{1,0:T(8,128)} %bitcast.9, f32[128,1024]{1,0:T(8,128)} %eig_h.1, f32[4,1,256]{2,1,0:T(1,128)} %bitcast.10, ...), custom_call_target="tpu_custom_call" | custom-call | tf_op jit(solution)/shard_map/pallas_call | solution.py:722
  60.6 0.6 copy.13
  61.2 0.7 %copy.14 = f32[512,64]{0,1:T(8,128)} copy(f32[512,64]{0,1:T(8,128)S(1)} %bitcast.7) | data formatting | bytes 262144

commit v3 on v2

--- a/solution.py
+++ b/solution.py
@@ -374,7 +374,7 @@
         hear()
 
     def e_place(t):
-        o = n - 1 - t
+        o = jnp.where(t < n // 2, n - 1 - t, t - n // 2 + 1)
         return lax.rem(b + lax.rem(o, nb), nb), at(lax.div(o, group), lax.rem(lax.div(o, nb), 2))
 
     def e_source(o):
@@ -460,6 +460,10 @@
 
     later(nz - 1)
     e_start(4)
+
+    @pl.loop(0, n - 1)
+    def _(t):
+        o_copy(t).start()
 
     a = feat[...]
     sa = jnp.sqrt(jnp.mean(a * a, axis=1, keepdims=True) + EPS)
@@ -496,10 +500,6 @@
     @pl.loop(1, nc)
     def _(t):
         r_copy(nc - t).start()
-
-    @pl.loop(0, n - 1)
-    def _(t):
-        o_copy(t).start()
 
     e_start(5)
 

time: 62 us -> 59.9 us (0.966)
  Pallas kernels: 59.9 us -> 57.9 us
    pallas_call x1, Pallas kernels: 59.9 us -> 57.9 us  [per_device(): pl.pallas_call(functools.partial(body, nb, nc), out_shape=(jax.ShapeDtype...]
where the time goes in v3:
time: 59.9 us; the launch traced here: 59.8 us
  Pallas kernels  57.9 us (97%)
  local copies, waits for them, and re-layouts  1.27 us (2%)
  between operations  0.64 us (1%)
    pallas_call x1, Pallas kernels, per_device(): pl.pallas_call(functools.partial(body, nb, nc), out_shape=(jax.ShapeDtype...  57.9 us
    unnamed x2, local copies, waits for them, and re-layouts  1.27 us

profile of v3, /device:TPU:0, one launch (start us, length us, event | category | flops | bytes accessed | tf_op | source)
XLA Modules:
  0.0 59.8 jit_solution(2828842549500508213)
XLA Ops:
  0.6 57.9 %shard_map.104 = (f32[64,64]{1,0:T(8,128)S(1)}, f32[64,512]{1,0:T(8,128)S(1)}) custom-call(f32[1024,128]{1,0:T(8,128)} %pool_f_h.1, f32[64,1024]{1,0:T(8,128)} %bitcast.8, s32[1,64]{1,0:T(1,128)} %bitcast.11, f32[512,128]{1,0:T(8,128)} %cen_h.1, f32[64,512]{1,0:T(8,128)} %bitcast.9, f32[128,1024]{1,0:T(8,128)} %eig_h.1, f32[4,1,256]{2,1,0:T(1,128)} %bitcast.10, ...), custom_call_target="tpu_custom_call" | custom-call | tf_op jit(solution)/shard_map/pallas_call | solution.py:722
  58.5 0.6 %copy.13 = f32[64,64]{1,0:T(8,128)} copy(f32[64,64]{1,0:T(8,128)S(1)} %get-tuple-element.8) | data formatting | bytes 32768
  59.1 0.7 %copy.14 = f32[512,64]{0,1:T(8,128)} copy(f32[512,64]{0,1:T(8,128)S(1)} %bitcast.7) | data formatting | bytes 262144

commit v4 on v3

--- a/solution.py
+++ b/solution.py
@@ -15,8 +15,7 @@
 MESH = pl.DeviceIdType.MESH
 LOW = jnp.bfloat16
 F32 = jnp.float32
-FAR = (8, 0, 0, 0, 0, 16)
-NEAR = (7, 0, 0, 0, 0, 16)
+INNER, OUTER = 8, 12
 ACOS = (
     1.5707963050,
     -0.2145988016,
@@ -374,7 +373,16 @@
         hear()
 
     def e_place(t):
-        o = jnp.where(t < n // 2, n - 1 - t, t - n // 2 + 1)
+        own_plane = t - (n - group) + 1
+        far_first = jnp.where(t < n // 2, n - 1 - t, t - n // 2 + group)
+        near_between = jnp.where(
+            t < n // 4,
+            n - 1 - t,
+            jnp.where(
+                t < 3 * n // 4 - group, t - n // 4 + group, n - 1 + n // 2 - group - t
+            ),
+        )
+        o = jnp.where(t >= n - group, own_plane, jnp.where(inner, far_first, near_between))
         return lax.rem(b + lax.rem(o, nb), nb), at(lax.div(o, group), lax.rem(lax.div(o, nb), 2))
 
     def e_source(o):
@@ -397,20 +405,15 @@
         db, dc = e_place(t)
         return copy(offsend.at[dc], offrx.at[mine], o_s.at[t], o_r.at[mine], db, dc)
 
-    marks_at = [0, n // 2]
-    ends_at = [n // 2, n - 1]
-
-    def e_start(step):
-        for kind, plan in enumerate((FAR, NEAR)):
-            lo, total = marks_at[kind], ends_at[kind]
-            hi = total if step == len(plan) - 1 else min(total, lo + plan[step] * n // 32)
-            marks_at[kind] = hi
-
-            @pl.loop(lo, hi)
-            def _(t):
-                e_copy(t).start()
-
-    e_start(0)
+    early = jnp.where(inner, INNER * (n - group) // 24, OUTER * (n - group) // 24)
+
+    def e_start(lo, hi):
+        @pl.loop(lo, hi)
+        def _(t):
+            e_copy(t).start()
+
+    e_start(n - group, n - 1)
+    e_start(0, early)
 
     def p_copy(t):
         s = at(lax.div(t, 2), lax.rem(t, 2))
@@ -430,11 +433,11 @@
         return fold(pred[:rows]), fold(pred[rows:])
 
     spread_end(feat_all, f_s, f_r, 0)
+    spread_pass(feat_all, f_s, f_r, 1)
     low, high = pair(0)
     prx[c] = jnp.where(y == 0, low, high)
     ppart[c ^ 1] = jnp.where(y == 0, high, low)
     p_copy(1).start()
-    e_start(1)
 
     def later(p):
         spread_end(feat_all, f_s, f_r, p)
@@ -445,13 +448,10 @@
         p_copy(2 * p).start()
         p_copy(2 * p + 1).start()
 
-    spread_pass(feat_all, f_s, f_r, 1)
     spread_pass(feat_all, f_s, f_r, 2)
     later(1)
-    e_start(2)
     spread_pass(feat_all, f_s, f_r, 3)
     later(2)
-    e_start(3)
 
     @pl.loop(3, nz - 1)
     def _(p):
@@ -459,7 +459,6 @@
         later(p)
 
     later(nz - 1)
-    e_start(4)
 
     @pl.loop(0, n - 1)
     def _(t):
@@ -501,7 +500,7 @@
     def _(t):
         r_copy(nc - t).start()
 
-    e_start(5)
+    e_start(early, n - group)
 
     res_v[...] = resid
     res_store = pltpu.make_async_copy(res_v, res_out, out_s.at[0])
@@ -602,20 +601,14 @@
     next(g_sum)
     ebar[...] = add_group(0)
     next(g_sum)
-    ebar[...] += add_group(1)
     next(g_sum)
-
-    def add_later(p):
+    gsplit = split(jnp.concatenate([gall[j] for j in range(4)], axis=1))
+
+    for p in range(nz - 1, 0, -1):
         ebar[...] += add_group(p)
 
-    for p in range(2, min(nz, 4)):
-        add_later(p)
-    for p in range(4, nz):
-        add_later(p)
-
-    g = jnp.concatenate([gall[j] for j in range(4)], axis=1)
     ebh, ebl = split(ebar[...])
-    coeff = dot3(split(g), (ebh, ebl), 1, 0)
+    coeff = dot3(gsplit, (ebh, ebl), 1, 0)
     og = outs // nc
     for j in range(nc):
         csend[j] = coeff[j * og : (j + 1) * og]

time: 59.9 us -> 59.3 us (0.990)
  Pallas kernels: 57.9 us -> 57.2 us
    pallas_call x1, Pallas kernels: 57.9 us -> 57.2 us  [per_device(): pl.pallas_call(functools.partial(body, nb, nc), out_shape=(jax.ShapeDtype...]
where the time goes in v4:
time: 59.3 us; the launch traced here: 59.1 us
  Pallas kernels  57.2 us (96%)
  local copies, waits for them, and re-layouts  1.27 us (2%)
  between operations  0.64 us (1%)
    pallas_call x1, Pallas kernels, per_device(): pl.pallas_call(functools.partial(body, nb, nc), out_shape=(jax.ShapeDtype...  57.2 us
    unnamed x2, local copies, waits for them, and re-layouts  1.27 us

profile of v4, /device:TPU:0, one launch (start us, length us, event | category | flops | bytes accessed | tf_op | source)
XLA Modules:
  0.0 59.1 jit_solution(18333748997419948674)
XLA Ops:
  0.6 57.2 %shard_map.104 = (f32[64,64]{1,0:T(8,128)S(1)}, f32[64,512]{1,0:T(8,128)S(1)}) custom-call(f32[1024,128]{1,0:T(8,128)} %pool_f_h.1, f32[64,1024]{1,0:T(8,128)} %bitcast.8, s32[1,64]{1,0:T(1,128)} %bitcast.11, f32[512,128]{1,0:T(8,128)} %cen_h.1, f32[64,512]{1,0:T(8,128)} %bitcast.9, f32[128,1024]{1,0:T(8,128)} %eig_h.1, f32[4,1,256]{2,1,0:T(1,128)} %bitcast.10, ...), custom_call_target="tpu_custom_call" | custom-call | tf_op jit(solution)/shard_map/pallas_call | solution.py:715
  57.9 0.6 %copy.13 = f32[64,64]{1,0:T(8,128)} copy(f32[64,64]{1,0:T(8,128)S(1)} %get-tuple-element.8) | data formatting | bytes 32768
  58.5 0.7 %copy.14 = f32[512,64]{0,1:T(8,128)} copy(f32[512,64]{0,1:T(8,128)S(1)} %bitcast.7) | data formatting | bytes 262144

commit v5 on v4

--- a/solution.py
+++ b/solution.py
@@ -652,12 +652,21 @@
     scaled = jnp.concatenate([call[j] for j in range(nc)], axis=0)
     u = dot3(split(scaled), (ebh, ebl), 1, 1)
     u_sum = reduce_parts(u, usend, urx, uown, uxrx, uall, u_s, u_r)
-    for _ in range(4):
+    for _ in range(3):
         next(u_sum)
-    for j in range(4):
-        upd_v[:, j * piece : (j + 1) * piece] = uall[j] - gall[j]
-    upd_store = pltpu.make_async_copy(upd_v, upd_out, out_s.at[1])
+
+    def store_half(h):
+        at_half = pl.ds(pl.multiple_of(h * 2 * piece, 2 * piece), 2 * piece)
+        upd_v[h] = jnp.concatenate(
+            [uall[2 * h + j] - gall[2 * h + j] for j in range(2)], axis=1
+        )
+        return pltpu.make_async_copy(upd_v.at[h], upd_out.at[:, at_half], out_s.at[1 + h])
+
+    upd_store = store_half(k2)
     upd_store.start()
+    next(u_sum)
+    upd_last = store_half(1 - k2)
+    upd_last.start()
 
     spread_sent(feat, feat_all, f_s, f_r)
 
@@ -677,6 +686,7 @@
     next(u_sum)
     res_store.wait()
     upd_store.wait()
+    upd_last.wait()
 
 
 def per_device(
@@ -732,7 +742,7 @@
             vm((1, pts), jnp.int32),
             vm((1, pts), jnp.int32),
             vm((rows, outs), F32),
-            vm((outs, cdev), F32),
+            vm((2, outs, cdev // 2), F32),
             vm((rows, dim), F32),
             vm((nc, rows, dim), F32),
             vm((cdev, 4 * dim), LOW),
@@ -757,7 +767,7 @@
             vm((nc, og, qb), F32),
         ]
         + reduced
-        + [dma((10,)), dma((2,)), pltpu.SemaphoreType.REGULAR((2,))]
+        + [dma((10,)), dma((3,)), pltpu.SemaphoreType.REGULAR((2,))]
         + pair * 3
         + every * 2
         + sums

time: 59.3 us -> 59.1 us (level)
  no operation moved by 1% of the time
where the time goes in v5:
time: 59.1 us; the launch traced here: 58.9 us
  Pallas kernels  57 us (96%)
  local copies, waits for them, and re-layouts  1.27 us (2%)
  between operations  0.64 us (1%)
    pallas_call x1, Pallas kernels, per_device(): pl.pallas_call(functools.partial(body, nb, nc), out_shape=(jax.ShapeDtype...  57 us
    unnamed x2, local copies, waits for them, and re-layouts  1.27 us

profile of v5, /device:TPU:0, one launch (start us, length us, event | category | flops | bytes accessed | tf_op | source)
XLA Modules:
  0.0 58.9 jit_solution(4647794318482474690)
XLA Ops:
  0.6 57.0 %shard_map.104 = (f32[64,64]{1,0:T(8,128)S(1)}, f32[64,512]{1,0:T(8,128)S(1)}) custom-call(f32[1024,128]{1,0:T(8,128)} %pool_f_h.1, f32[64,1024]{1,0:T(8,128)} %bitcast.8, s32[1,64]{1,0:T(1,128)} %bitcast.11, f32[512,128]{1,0:T(8,128)} %cen_h.1, f32[64,512]{1,0:T(8,128)} %bitcast.9, f32[128,1024]{1,0:T(8,128)} %eig_h.1, f32[4,1,256]{2,1,0:T(1,128)} %bitcast.10, ...), custom_call_target="tpu_custom_call" | custom-call | tf_op jit(solution)/shard_map/pallas_call | solution.py:725
  57.7 0.6 %copy.13 = f32[64,64]{1,0:T(8,128)} copy(f32[64,64]{1,0:T(8,128)S(1)} %get-tuple-element.8) | data formatting | bytes 32768
  58.3 0.7 %copy.14 = f32[512,64]{0,1:T(8,128)} copy(f32[512,64]{0,1:T(8,128)S(1)} %bitcast.7) | data formatting | bytes 262144
